TPU v7x, 128 devices: a whole 4x4x4 slice. The times are simulated.
128 devices in a mesh: wide: 16 (over y, x), narrow: 8 (over z, core).
Axes of the slice: x: 4, y: 4, z: 4, core: 2. Of those that a mesh axis runs over, the one named last changes fastest.
Arguments:
- diag_block: float32 [256, 256], P('narrow'), as said below
- panel_below: float32 [24576, 256], P(('wide', 'narrow')), may hold values from -0.216 to 0.216
- trailing_slab: float32 [12288, 24576], P('narrow', 'wide'), may hold values from -6 to 6
Outputs:
- updated: float32 [12288, 24576], P('narrow', 'wide')
Inputs may be any that keep to these rules, and one draw needn't show every extreme that they name: `diag_block`: symmetric positive definite; its smallest eigenvalue is 0.01 or more and its diagonal entries lie between 0.4 and 2.1.
All inputs are finite; a program needn't handle non-finite values.
Results may differ from a plain program's by a relative error of at most 0.00016.
Values sent between devices are 32-bit elements; how exact they have to be, the bound alone decides.
A program may use at most 64 MiB of HBM per device.

v0:
```python
import jax
import jax.numpy as jnp
from jax import lax
from jax.sharding import PartitionSpec as P

unit_gamma = 65538.0 * 2.0 ** (-24) / (1.0 - 65538.0 * 2.0 ** (-24))


def from_root(block, axis, source):
    block = jnp.where(lax.axis_index(axis) == source, block, jnp.zeros_like(block))
    return lax.psum(block, axis)


def factor_block(diag_full):
    trace_sum = jnp.sum(jnp.diagonal(diag_full))
    shift_value = unit_gamma * trace_sum / diag_full.shape[0]
    identity = jnp.eye(diag_full.shape[0], dtype=jnp.float32)
    return jnp.linalg.cholesky(diag_full - shift_value * identity)


def solve_rows(raw_panel, lower_factor):
    return jax.scipy.linalg.solve_triangular(lower_factor, raw_panel.T, lower=True).T


def on_device(diag_block, panel_below, trailing_slab):
    diag_full = lax.all_gather(diag_block, "narrow", axis=0, tiled=True)
    lower_factor = factor_block(diag_full)
    owner = lax.axis_index("narrow")
    solved_mine = solve_rows(panel_below, lower_factor)
    column_panel = lax.all_gather(solved_mine, "narrow", axis=0, tiled=True)
    row_panel = from_root(column_panel, "wide", owner)
    product = lax.dot_general(
        row_panel,
        column_panel,
        (((1,), (1,)), ((), ())),
        precision=lax.Precision.HIGHEST,
        preferred_element_type=jnp.float32,
    )
    return trailing_slab - product


def solution(mesh):
    placed = (P("narrow", None), P(("wide", "narrow"), None), P("narrow", "wide"))
    return jax.shard_map(
        on_device, mesh=mesh, in_specs=placed, out_specs=P("narrow", "wide"), check_vma=False
    )
```

profile of v0, /device:TPU:0, one launch (start us, length us, event | category | flops | bytes accessed | tf_op | source)
XLA Modules:
  0.0 223.8 jit_solution(3834586539519067064)
XLA Ops:
  6.6 14.3 %all_gather.6 = f32[256,256]{1,0:T(8,128)S(1)} all-gather(f32[32,256]{1,0:T(8,128)} %param.3), channel_id=1, replica_groups=mesh['wide'=16,'narrow'=8] {'narrow'}, dimensions={0}, use_global_device_ids=true | all-gather | bytes 294912 | tf_op jit(solution)/shard_map/all_gather | solution.py:26
  21.0 2.3 %gather_fusion = f32[256]{0:T(256)S(1)} fusion(f32[256,256]{1,0:T(8,128)S(1)} %all_gather.6, s32[256]{0:T(256)S(1)} %bitcast.35), kind=kCustom, calls=%fused_computation | custom fusion | bytes 4096 | tf_op jit(solution)/shard_map/jit(diagonal)/cond/branch_0_fun/gather | solution.py:15
  23.4 0.6 reduce_sum.9
  24.7 0.1 copy.24
  24.9 11.7 %cholesky.49 = f32[128,128]{1,0:T(8,128)S(1)} custom-call(f32[128,128]{1,0:T(8,128)S(1)} %cholesky.115), custom_call_target="Cholesky" | custom-call | tf_op jit(solution)/shard_map/jit(cholesky)/cholesky | solution.py:18
  36.7 9.8 %custom-call.15 = f32[1,128,128]{1,2,0:T(8,128)S(1)} custom-call(f32[1,128,128]{2,1,0:T(8,128)S(1)} %get-tuple-element.40), custom_call_target="InvertDiagBlocksLowerTriangular" | custom-call | tf_op jit(solution)/shard_map/jit(cholesky)/cholesky | solution.py:18
  46.5 0.2 fusion.5
  46.7 0.3 convolution_subtract_fusion.2
  47.1 11.7 %cholesky.103 = f32[128,128]{1,0:T(8,128)S(1)} custom-call(f32[128,128]{1,0:T(8,128)S(1)} %convolution_subtract_fusion.2), custom_call_target="Cholesky" | custom-call | tf_op jit(solution)/shard_map/jit(cholesky)/cholesky | solution.py:18
  59.0 0.7 compare_reduce_fusion
  61.1 4.3 %while.1 = (s32[]{:T(128)}, f32[256,256]{0,1:T(8,128)S(1)}, s32[2,2]{1,0:T(2,128)S(1)}, f32[2,128,128]{2,1,0:T(8,128)S(1)}, s32[]{:T(128)}) while((s32[]{:T(128)}, f32[256,256]{0,1:T(8,128)S(1)}, s32[2,2]{1,0:T(2,128)S(1)}, f32[2,128,128]{2,1,0:T(8,128)S(1)}, s32[]{:T(128)}) %tuple.25), condition=%wide.while_cond, body=%wide.while_body.sunk | while | flops 2 | bytes 393329 | solution.py:22
  61.1 0.7 fusion.16
  61.8 1.3 dynamic-slice.7
  63.3 0.7 fusion.16
  63.9 1.3 dynamic-slice.7
  65.4 19.9 %custom-call.16 = f32[2,128,128]{1,2,0:T(8,128)S(1)} custom-call(f32[2,128,128]{2,1,0:T(8,128)S(1)} %get-tuple-element.12), custom_call_target="InvertDiagBlocksLowerTriangular" | custom-call | tf_op jit(solution)/shard_map/jit(_solve_triangular)/triangular_solve | solution.py:22
  85.3 0.2 fusion.1
  85.5 0.2 convolution_subtract_fusion.1
  85.8 0.2 fusion.4
  86.0 0.7 maximum_bitcast_fusion
  86.8 25.8 %all-gather.2.cloned.1.call-done = f32[1536,256]{1,0:T(8,128)} async-done(((f32[192,256]{1,0:T(8,128)}), f32[1536,256]{1,0:T(8,128)}) %all-gather.2.cloned.1.call-update) | async-done | bytes 1572880 | tf_op jit(solution)/shard_map/all_gather | solution.py:30
  112.6 2.7 %broadcast_select_fusion = f32[1536,256]{1,0:T(8,128)} fusion(f32[1536,256]{1,0:T(8,128)} %all-gather.2.cloned.1.call-done, pred[]{:T(512)S(6)} %eq.6), kind=kLoop, calls=%fused_computation.6 | loop fusion | flops 393216 | bytes 3145729 | tf_op jit(solution)/shard_map/jit(_where)/select_n | solution.py:10
  115.3 89.2 %all-reduce.3.cloned.1.call-done = f32[1536,256]{1,0:T(8,128)} async-done(((f32[1536,256]{1,0:T(8,128)}), f32[1536,256]{1,0:T(8,128)}) %all-reduce.3.cloned.1.call-update) | async-done | bytes 1572880 | tf_op jit(solution)/shard_map/psum | solution.py:11
  204.5 12.4 %convolution_subtract_fusion = f32[1536,1536]{1,0:T(8,128)} fusion(f32[1536,1536]{1,0:T(8,128)} %param.5, f32[1536,256]{1,0:T(8,128)} %all-reduce.3.cloned.1.call-done, f32[1536,256]{1,0:T(8,128)S(1)} %copy-done), kind=kOutput, calls=%fused_computation.3 | convolution fusion | flops 7250116608 | bytes 22020096 | tf_op jit(solution)/shard_map/dot_general | solution.py:32
  (31 shorter events, 1.0 us)
Async XLA Ops:
  6.5 106.1 %all-gather.2.cloned.1.call-start = ((), (), s32[]{:S(2)}) async-start(), calls=%async_computation | async-start | bytes 1769472 | tf_op jit(solution)/shard_map/all_gather | solution.py:30
  59.0 26.3 %copy-start.1 = (f32[192,256]{1,0:T(8,128)S(1)}, f32[192,256]{1,0:T(8,128)}, u32[]{:S(2)}) copy-start(f32[192,256]{1,0:T(8,128)} %param.4) | copy-start | bytes 589828
  86.7 117.7 %all-reduce.3.cloned.1.call-start = ((), (), s32[]{:S(2)}) async-start(), calls=%async_computation.1 | async-start | bytes 3145728 | tf_op jit(solution)/shard_map/psum | solution.py:11
  115.3 89.2 %copy-start = (f32[1536,256]{1,0:T(8,128)S(1)}, f32[1536,256]{1,0:T(8,128)}, u32[]{:S(2)}) copy-start(f32[1536,256]{1,0:T(8,128)} %all-gather.2.cloned.1.call-done) | copy-start | bytes 4718596
Sparse Core Ops, SparseCore 0:
  86.9 25.7 all-gather.1
  115.9 88.5 all-reduce.2
where the time goes:
time: 224 us
  waiting for transfers between devices  115 us (51%)
  other arithmetic  57.9 us (26%)
  between operations  15.5 us (7%)
  blocking collectives  14.3 us (6%)
  matrix products  13.6 us (6%)
  local copies, waits for them, and re-layouts  7.22 us (3%)
    psum x1, waiting for transfers between devices, from_root(): return lax.psum(block, axis)  89.2 us
    another operation x6, other arithmetic, factor_block(): return jnp.linalg.cholesky(diag_full - shift_value * identity)  34 us
    all_gather x1, waiting for transfers between devices, on_device(): column_panel = lax.all_gather(solved_mine, 'narrow', axis=0, tiled=True)  25.8 us
    another operation x3, other arithmetic, solve_rows(): jax.scipy.linalg.solve_triangular(lower_factor, raw_panel.T, lower=True)  19.9 us
    all_gather x1, blocking collectives, on_device(): diag_full = lax.all_gather(diag_block, 'narrow', axis=0, tiled=True)  14.3 us
    dot_general x1, matrix products, on_device(): lax.dot_general(row_panel, column_panel, (((1,), (1,)), ((), ())), precis...  12.4 us
  transfers between devices with their start and end apart: 2, of which 2 were waited for; matrix products, arithmetic and copies ran while one was open for 0% of the time, Pallas kernels for 0%

commit v1 on v0

--- a/solution.py
+++ b/solution.py
@@ -8,7 +8,7 @@
 
 def from_root(block, axis, source):
     block = jnp.where(lax.axis_index(axis) == source, block, jnp.zeros_like(block))
-    return lax.psum(block, axis)
+    return jnp.sum(lax.all_gather(block, axis), axis=0)
 
 
 def factor_block(diag_full):

time: 224 us -> 298 us (1.33)
  waiting for transfers between devices: 115 us -> 179 us
  other arithmetic: 57.9 us -> 67.3 us
    all_gather x0 -> x1, waiting for transfers between devices: none -> 154 us  [from_root(): return jnp.sum(lax.all_gather(block, axis), axis=0)]
    psum x1 -> x0, waiting for transfers between devices: 89.2 us -> none  [from_root(): return lax.psum(block, axis)]
    reduce_sum x0 -> x1, other arithmetic: none -> 9.39 us  [from_root(): return jnp.sum(lax.all_gather(block, axis), axis=0)]
where the time goes in v1:
time: 298 us; the launch traced here: 297 us
  waiting for transfers between devices  179 us (60%)
  other arithmetic  67.3 us (23%)
  between operations  15.5 us (5%)
  blocking collectives  14.3 us (5%)
  matrix products  13.1 us (4%)
  local copies, waits for them, and re-layouts  7.22 us (2%)
    all_gather x1, waiting for transfers between devices, from_root(): return jnp.sum(lax.all_gather(block, axis), axis=0)  154 us
    another operation x6, other arithmetic, factor_block(): return jnp.linalg.cholesky(diag_full - shift_value * identity)  34 us
    all_gather x1, waiting for transfers between devices, on_device(): column_panel = lax.all_gather(solved_mine, 'narrow', axis=0, tiled=True)  25.8 us
    another operation x3, other arithmetic, solve_rows(): jax.scipy.linalg.solve_triangular(lower_factor, raw_panel.T, lower=True)  19.9 us
    all_gather x1, blocking collectives, on_device(): diag_full = lax.all_gather(diag_block, 'narrow', axis=0, tiled=True)  14.3 us
    dot_general x1, matrix products, on_device(): lax.dot_general(row_panel, column_panel, (((1,), (1,)), ((), ())), precis...  12 us
    reduce_sum x1, other arithmetic, from_root(): return jnp.sum(lax.all_gather(block, axis), axis=0)  9.39 us
  transfers between devices with their start and end apart: 2, of which 2 were waited for; matrix products, arithmetic and copies ran while one was open for 0% of the time, Pallas kernels for 0%

profile of v1, /device:TPU:0, one launch (start us, length us, event | category | flops | bytes accessed | tf_op | source)
XLA Modules:
  0.0 297.1 jit_solution(754772144670188619)
XLA Ops:
  6.6 14.3 %all_gather.12 = f32[256,256]{1,0:T(8,128)S(1)} all-gather(f32[32,256]{1,0:T(8,128)} %param.3), channel_id=1, replica_groups=mesh['wide'=16,'narrow'=8] {'narrow'}, dimensions={0}, use_global_device_ids=true | all-gather | bytes 294912 | tf_op jit(solution)/shard_map/all_gather | solution.py:26
  21.0 2.3 gather_fusion
  23.4 0.6 reduce_sum.18
  24.9 11.7 %cholesky.49 = f32[128,128]{1,0:T(8,128)S(1)} custom-call(f32[128,128]{1,0:T(8,128)S(1)} %cholesky.115), custom_call_target="Cholesky" | custom-call | tf_op jit(solution)/shard_map/jit(cholesky)/cholesky | solution.py:18
  36.7 9.8 %custom-call.15 = f32[1,128,128]{1,2,0:T(8,128)S(1)} custom-call(f32[1,128,128]{2,1,0:T(8,128)S(1)} %get-tuple-element.40), custom_call_target="InvertDiagBlocksLowerTriangular" | custom-call | tf_op jit(solution)/shard_map/jit(cholesky)/cholesky | solution.py:18
  46.5 0.2 fusion.5
  46.7 0.3 convolution_subtract_fusion.2
  47.1 11.7 %cholesky.103 = f32[128,128]{1,0:T(8,128)S(1)} custom-call(f32[128,128]{1,0:T(8,128)S(1)} %convolution_subtract_fusion.2), custom_call_target="Cholesky" | custom-call | tf_op jit(solution)/shard_map/jit(cholesky)/cholesky | solution.py:18
  59.0 0.7 compare_reduce_fusion
  61.1 4.3 %while.1 = (s32[]{:T(128)}, f32[256,256]{0,1:T(8,128)S(1)}, s32[2,2]{1,0:T(2,128)S(1)}, f32[2,128,128]{2,1,0:T(8,128)S(1)}, s32[]{:T(128)}) while((s32[]{:T(128)}, f32[256,256]{0,1:T(8,128)S(1)}, s32[2,2]{1,0:T(2,128)S(1)}, f32[2,128,128]{2,1,0:T(8,128)S(1)}, s32[]{:T(128)}) %tuple.25), condition=%wide.while_cond, body=%wide.while_body.sunk | while | flops 2 | bytes 393329 | solution.py:22
  61.1 0.7 fusion.16
  61.8 1.3 dynamic-slice.7
  63.3 0.7 fusion.16
  63.9 1.3 dynamic-slice.7
  65.4 19.9 %custom-call.16 = f32[2,128,128]{1,2,0:T(8,128)S(1)} custom-call(f32[2,128,128]{2,1,0:T(8,128)S(1)} %get-tuple-element.12), custom_call_target="InvertDiagBlocksLowerTriangular" | custom-call | tf_op jit(solution)/shard_map/jit(_solve_triangular)/triangular_solve | solution.py:22
  85.3 0.2 fusion.1
  85.5 0.2 convolution_subtract_fusion.1
  85.8 0.2 fusion.4
  86.0 0.7 maximum_bitcast_fusion
  86.8 25.8 %all-gather.4.cloned.1.call-done = f32[1536,256]{1,0:T(8,128)} async-done(((f32[192,256]{1,0:T(8,128)}), f32[1536,256]{1,0:T(8,128)}) %all-gather.4.cloned.1.call-update) | async-done | bytes 1572880 | tf_op jit(solution)/shard_map/all_gather | solution.py:30
  112.6 2.7 broadcast_select_fusion
  115.3 153.6 %all-gather.6.cloned.1.call-done = f32[24576,256]{1,0:T(8,128)} async-done(((f32[1536,256]{1,0:T(8,128)}), f32[24576,256]{1,0:T(8,128)}) %all-gather.6.cloned.1.call-update) | async-done | bytes 25165840 | tf_op jit(solution)/shard_map/all_gather | solution.py:11
  268.9 9.4 %reduce_sum.19 = f32[1536,256]{1,0:T(8,128)S(1)} reduce(f32[16,1536,256]{2,1,0:T(8,128)} %bitcast.36, f32[]{:T(128)} %constant.95.clone.1), dimensions={0}, to_apply=%region_5.6 | reduce | flops 5898240 | bytes 26738692 | tf_op jit(solution)/shard_map/reduce_sum | solution.py:11
  278.3 12.0 %convolution_subtract_fusion = f32[1536,1536]{1,0:T(8,128)} fusion(f32[1536,1536]{1,0:T(8,128)} %param.5, f32[1536,256]{1,0:T(8,128)S(1)} %reduce_sum.19, f32[1536,256]{1,0:T(8,128)S(1)} %copy-done), kind=kOutput, calls=%fused_computation.3 | convolution fusion | flops 7250116608 | bytes 22020096 | tf_op jit(solution)/shard_map/dot_general | solution.py:32
  (32 shorter events, 1.1 us)
Async XLA Ops:
  6.5 106.1 %all-gather.4.cloned.1.call-start = ((), (), s32[]{:S(2)}) async-start(), calls=%async_computation | async-start | bytes 1769472 | tf_op jit(solution)/shard_map/all_gather | solution.py:30
  59.0 26.3 %copy-start.1 = (f32[192,256]{1,0:T(8,128)S(1)}, f32[192,256]{1,0:T(8,128)}, u32[]{:S(2)}) copy-start(f32[192,256]{1,0:T(8,128)} %param.4) | copy-start | bytes 589828
  86.7 182.2 %all-gather.6.cloned.1.call-start = ((), (), s32[]{:S(2)}) async-start(), calls=%async_computation.1 | async-start | bytes 26738688 | tf_op jit(solution)/shard_map/all_gather | solution.py:11
  268.9 9.4 %copy-start = (f32[1536,256]{1,0:T(8,128)S(1)}, f32[1536,256]{1,0:T(8,128)}, u32[]{:S(2)}) copy-start(f32[1536,256]{1,0:T(8,128)} %all-gather.4.cloned.1.call-done) | copy-start | bytes 4718596
Sparse Core Ops, SparseCore 0:
  86.9 25.7 all-gather.3
  115.4 153.4 all-gather.5
